TPU v7x, 256 devices: a whole 4x4x8 slice. The times are simulated.
256 devices in a mesh: pair: 4 (over y), ep: 64 (over x, z, core).
Axes of the slice: x: 4, y: 4, z: 8, core: 2. Of those that a mesh axis runs over, the one named last changes fastest.
Arguments:
- hidden: float32 [4, 2048, 2048], P('pair', 'ep'), may hold values from -6 to 6
- moe_gain: float32 [2048], replicated, may hold values from 0.25 to 1.75
- expert_ids: int32 [4, 2048, 2], P('pair', 'ep'), may hold values from 0 to 31, all different within a row; in each aligned block of 32 rows (0 to 31, 32 to 63, ..., all dimensions but the last counted through in order) at most 4 rows name the same one
- gate_weights: float32 [4, 2048, 2], P('pair', 'ep'), may hold values from 0.2 to 1
- w_gate: bfloat16 [64, 2048, 2048], P('ep', None, 'pair'), may hold values from -0.125 to 0.125
- w_up: bfloat16 [64, 2048, 2048], P('ep', None, 'pair'), may hold values from -0.125 to 0.125
- w_down: bfloat16 [64, 2048, 2048], P('ep', 'pair'), may hold values from -0.09375 to 0.09375
- final_gain: float32 [2048], replicated, may hold values from 0.25 to 1.75
- w_out: bfloat16 [2048, 128], replicated, may hold values from -0.125 to 0.125
- latent: float32 [4, 2048, 64], P('pair', 'ep'), may hold values from -6 to 6
- w_in: bfloat16 [128, 2048], replicated, may hold values from -0.5 to 0.5
- modulation: float32 [4, 2, 2048], P('pair'), may hold values from -3 to 16, as said below
- w_qkv: bfloat16 [2048, 3072], P(None, 'pair'), may hold values from -0.125 to 0.125
Outputs:
- latent_next: float32 [4, 2048, 64], P('pair', 'ep')
- attended: bfloat16 [4, 2048, 1024], P('pair', 'ep')
Inputs may be any that keep to these rules, and one draw needn't show every extreme that they name: `expert_ids`: within the 32 frames of each device no expert is named more than 4 times, a bound that some block reaches; the two experts of a frame differ. `modulation`: row 0 is a shift, row 1 a positive scale.
All inputs are finite; a program needn't handle non-finite values.
Results may differ from a plain program's by a relative error of at most 0.03.
Values may be sent and summed in bfloat16 or wider, within the bound.
No kernel may reach another device: no remote copies, remote signals or barrier semaphores. Data moves between devices by JAX's collectives and lax.ppermute only.
A program may use at most 64 MiB of HBM per device.

v0:
```python
import math

import jax
import jax.numpy as jnp
from jax import lax
from jax.sharding import PartitionSpec as P

HDIM = 128


EPSILON = 1e-06
GUIDANCE = 3.0
STEP_SIZE = 0.25


def from_partner(value, axis, bit):
    mask = 2**bit
    pairs = [(source, source ^ mask) for source in range(lax.axis_size(axis))]
    return lax.ppermute(value, axis, pairs)


def rms_scale(values):
    return values * lax.rsqrt(jnp.mean(values * values, -1, keepdims=True) + EPSILON)


def per_device(
    hidden,
    moe_gain,
    expert_ids,
    gate_weights,
    w_gate,
    w_up,
    w_down,
    final_gain,
    w_out,
    latent,
    w_in,
    modulation,
    w_qkv,
):
    tok_rows = hidden.shape[1]
    model_width = hidden.shape[2]
    experts = lax.axis_size("ep") // 2
    capacity = 4 * tok_rows // experts
    slot_count = experts * capacity
    own_hidden = hidden[0]
    normed = (rms_scale(own_hidden) * moe_gain).astype(jnp.bfloat16)
    flat_ids = expert_ids[0].reshape(-1)
    onehot = (flat_ids[:, None] == jnp.arange(experts, dtype=jnp.int32)[None, :]).astype(jnp.int32)
    slot_rank = jnp.sum((jnp.cumsum(onehot, 0) - onehot) * onehot, 1)
    places = flat_ids * capacity + slot_rank
    matches = places[None, :] == jnp.arange(slot_count, dtype=jnp.int32)[:, None]
    dispatch_mat = jnp.sum(matches.reshape(slot_count, tok_rows, 2).astype(jnp.float32), 2).astype(
        jnp.bfloat16
    )
    buffers = jnp.dot(dispatch_mat, normed, preferred_element_type=jnp.float32).astype(jnp.bfloat16)
    doubled = jnp.broadcast_to(
        buffers.reshape(experts, 1, capacity, model_width), (experts, 2, capacity, model_width)
    ).reshape(2 * experts, capacity, model_width)
    arrived = lax.all_to_all(doubled, "ep", split_axis=0, concat_axis=0, tiled=True)
    all_rows = lax.all_gather(arrived.reshape(-1, model_width), "pair", axis=0, tiled=True)
    gate_mat = w_gate[0]
    up_mat = w_up[0]
    down_mat = w_down[0]
    gated = jnp.dot(all_rows, gate_mat, preferred_element_type=jnp.float32)
    upward = jnp.dot(all_rows, up_mat, preferred_element_type=jnp.float32)
    active = (jax.nn.silu(gated) * upward).astype(jnp.bfloat16)
    halves = lax.psum_scatter(
        jnp.dot(active, down_mat, preferred_element_type=jnp.float32).astype(jnp.bfloat16),
        "pair",
        scatter_dimension=0,
        tiled=True,
    )
    returned = lax.all_to_all(
        halves.reshape(2 * experts, capacity, model_width),
        "ep",
        split_axis=0,
        concat_axis=0,
        tiled=True,
    )
    paired = returned.reshape(experts, 2, capacity, model_width)
    summed = (paired[:, 0].astype(jnp.float32) + paired[:, 1].astype(jnp.float32)).reshape(
        slot_count, model_width
    )
    combine_mat = jnp.sum(
        jnp.where(matches, gate_weights[0].reshape(-1)[None, :], 0.0).reshape(
            slot_count, tok_rows, 2
        ),
        2,
    )
    mixed_out = jnp.einsum("st,sd->td", combine_mat, summed, precision=lax.Precision.HIGHEST)
    resid = own_hidden + mixed_out
    velocity = jnp.dot(
        (rms_scale(resid) * final_gain).astype(jnp.bfloat16),
        w_out,
        preferred_element_type=jnp.float32,
    )
    own_latent = latent[0]
    outgoing = jnp.concatenate([velocity, own_latent], 1)
    incoming = from_partner(outgoing, "pair", 0)
    channels = velocity.shape[1]
    partner_vel = incoming[:, :channels]
    partner_latent = incoming[:, channels:]
    is_cond = lax.axis_index("pair") % 2 == 0
    cond_vel = jnp.where(is_cond, velocity, partner_vel)
    uncond_vel = jnp.where(is_cond, partner_vel, velocity)
    guided = uncond_vel + GUIDANCE * (cond_vel - uncond_vel)
    whole_latent = jnp.where(
        is_cond,
        jnp.concatenate([own_latent, partner_latent], 1),
        jnp.concatenate([partner_latent, own_latent], 1),
    )
    advanced = whole_latent + STEP_SIZE * guided
    half_width = own_latent.shape[1]
    own_next = jnp.where(is_cond, advanced[:, :half_width], advanced[:, half_width:])
    embedded = jnp.dot(advanced.astype(jnp.bfloat16), w_in, preferred_element_type=jnp.float32)
    modulated = (rms_scale(embedded) * modulation[0, 1] + modulation[0, 0]).astype(jnp.bfloat16)
    all_modulated = lax.all_gather(modulated, "pair", axis=0, tiled=True)
    local_cols = jnp.dot(all_modulated, w_qkv, preferred_element_type=jnp.float32).astype(
        jnp.bfloat16
    )
    projected = lax.all_to_all(local_cols, "pair", split_axis=0, concat_axis=1, tiled=True)
    head_width = projected.shape[1] // 3
    head_count = head_width // HDIM
    queries = projected[:, :head_width].reshape(tok_rows, head_count, HDIM)
    key_cols = projected[:, head_width : 2 * head_width]
    value_cols = projected[:, 2 * head_width :]
    score_scale = 1.0 / math.sqrt(HDIM)
    running_max = jnp.full((head_count, tok_rows), -1e30, jnp.float32)
    key_piece = lax.all_gather(key_cols, "ep", axis=0, tiled=True).reshape(-1, head_count, HDIM)
    value_piece = lax.all_gather(value_cols, "ep", axis=0, tiled=True).reshape(-1, head_count, HDIM)
    scores = (
        jnp.einsum("thd,nhd->htn", queries, key_piece, preferred_element_type=jnp.float32)
        * score_scale
    )
    new_max = jnp.maximum(running_max, jnp.max(scores, 2))
    weights = jnp.exp(scores - new_max[:, :, None])
    new_sum = jnp.sum(weights, 2)
    new_accum = jnp.einsum(
        "htn,nhd->htd", weights, value_piece.astype(jnp.float32), precision=lax.Precision.HIGHEST
    )
    attended = (
        (new_accum / new_sum[:, :, None])
        .transpose(1, 0, 2)
        .reshape(tok_rows, head_width)
        .astype(jnp.bfloat16)
    )
    return (own_next[None], attended[None])


def solution(mesh):
    return jax.shard_map(
        per_device,
        mesh=mesh,
        in_specs=(
            P("pair", "ep", None),
            P(),
            P("pair", "ep", None),
            P("pair", "ep", None),
            P("ep", None, "pair"),
            P("ep", None, "pair"),
            P("ep", "pair", None),
            P(),
            P(),
            P("pair", "ep", None),
            P(),
            P("pair", None, None),
            P(None, "pair"),
        ),
        out_specs=(P("pair", "ep", None), P("pair", "ep", None)),
        check_vma=False,
    )
```

profile of v0, /device:TPU:1, one launch (start us, length us, event | category | flops | bytes accessed | tf_op | source)
XLA Modules:
  0.0 427.8 jit_solution(2580671043403832083)
XLA Ops:
  7.2 0.9 copy.41
  8.8 0.7 bitcast_add_fusion
  9.5 1.1 fusion.15
  10.6 0.8 convert_reduce_fusion
  11.3 2.1 convolution_convert_fusion.1
  13.4 2.0 broadcast_in_dim.41
  15.5 1.5 broadcast_in_dim.42
  17.0 41.4 %all_to_all.29 = bf16[64,4,2048]{2,1,0:T(4,128)(2,1)} all-to-all(bf16[64,4,2048]{2,1,0:T(4,128)(2,1)S(1)} %bitcast.67), channel_id=1, replica_groups=mesh['pair'=4,'ep'=64] {'ep'}, dimensions={0} | all-to-all | bytes 2097152 | tf_op jit(solution)/shard_map/all_to_all | solution.py:60
  58.4 2.1 reshape.117
  60.7 47.7 %all-gather.4.cloned.1.call-done = bf16[1024,2048]{1,0:T(8,128)(2,1)} async-done(((bf16[256,2048]{1,0:T(8,128)(2,1)}), bf16[1024,2048]{1,0:T(8,128)(2,1)}) %all-gather.4.cloned.1.call-update) | async-done | bytes 4194320 | tf_op jit(solution)/shard_map/all_gather | solution.py:61
  108.4 6.6 %fusion.1 = f32[1024,512]{1,0:T(8,128)} fusion(bf16[1024,2048]{1,0:T(8,128)(2,1)} %all-gather.4.cloned.1.call-done, bf16[1,2048,512]{2,1,0:T(8,128)(2,1)} %param.18), kind=kOutput, calls=%fused_computation.5 | convolution fusion | flops 2147483648 | bytes 8388608 | tf_op jit(solution)/shard_map/dot_general | solution.py:66
  115.0 10.7 %convolution_convert_fusion = bf16[1024,2048]{1,0:T(8,128)(2,1)} fusion(bf16[1,512,2048]{2,1,0:T(8,128)(2,1)} %param.19, f32[1024,512]{1,0:T(8,128)} %fusion.1, bf16[1024,2048]{1,0:T(8,128)(2,1)} %all-gather.4.cloned.1.call-done, bf16[1,2048,512]{2,1,0:T(8,128)(2,1)} %param.17), kind=kOutput, calls=%fused_computation | convolution fusion | flops 4300210176 | bytes 14680064 | tf_op jit(solution)/shard_map/dot_general | solution.py:69
  125.7 50.0 %reduce-scatter.2.cloned.1.call-done = bf16[256,2048]{1,0:T(8,128)(2,1)} async-done(((bf16[1024,2048]{1,0:T(8,128)(2,1)}), bf16[256,2048]{1,0:T(8,128)(2,1)}) %reduce-scatter.2.cloned.1.call-update) | async-done | bytes 1048592 | tf_op jit(solution)/shard_map/reduce_scatter | solution.py:68
  175.7 2.3 reshape.118
  178.0 39.2 %all_to_all.30 = bf16[64,4,2048]{2,1,0:T(4,128)(2,1)S(1)} all-to-all(bf16[64,4,2048]{2,1,0:T(4,128)(2,1)} %reshape.118), channel_id=1, replica_groups=mesh['pair'=4,'ep'=64] {'ep'}, dimensions={0} | all-to-all | bytes 2097152 | tf_op jit(solution)/shard_map/all_to_all | solution.py:74
  217.2 1.3 convert_add_fusion
  218.5 2.6 add.72
  221.2 2.0 multiply_reduce_fusion.1
  223.2 1.3 fusion.18
  224.7 2.7 collective-permute-done
  227.5 1.4 multiply_reduce_fusion
  229.0 9.9 %all_gather.13 = bf16[128,2048]{1,0:T(8,128)(2,1)S(1)} all-gather(bf16[32,2048]{1,0:T(8,128)(2,1)S(1)} %add_convert_fusion), channel_id=1, replica_groups=mesh['pair'=4,'ep'=64] {'pair'}, dimensions={0}, use_global_device_ids=true | all-gather | bytes 655360 | tf_op jit(solution)/shard_map/all_gather | solution.py:118
  239.5 8.0 %all_to_all.31 = bf16[4,32,768]{2,1,0:T(8,128)(2,1)S(1)} all-to-all(bf16[4,32,768]{2,1,0:T(8,128)(2,1)S(1)} %bitcast.71), channel_id=1, replica_groups=mesh['pair'=4,'ep'=64] {'pair'}, dimensions={0} | all-to-all | bytes 393216 | tf_op jit(solution)/shard_map/all_to_all | solution.py:122
  247.5 0.7 slice_bitcast_fusion
  248.8 0.7 fusion.27
  249.5 78.2 %all-gather.6.cloned.1.call-done = bf16[2048,1024]{1,0:T(8,128)(2,1)} async-done(((bf16[32,1024]{1,0:T(8,128)(2,1)}), bf16[2048,1024]{1,0:T(8,128)(2,1)}) %all-gather.6.cloned.1.call-update) | async-done | bytes 4194320 | tf_op jit(solution)/shard_map/all_gather | solution.py:130
  327.7 6.5 %copy.44 = bf16[2048,1024]{0,1:T(8,128)(2,1)} copy(bf16[2048,1024]{1,0:T(8,128)(2,1)} %all-gather.6.cloned.1.call-done) | data formatting | bytes 8388608 | tf_op jit(solution)/shard_map/all_gather | solution.py:130
  334.1 2.9 fusion.34
  337.1 1.4 copy-done.1
  338.9 68.2 %all-gather.8.cloned.1.call-done = bf16[2048,1024]{1,0:T(8,128)(2,1)} async-done(((bf16[32,1024]{1,0:T(8,128)(2,1)}), bf16[2048,1024]{1,0:T(8,128)(2,1)}) %all-gather.8.cloned.1.call-update) | async-done | bytes 4194320 | tf_op jit(solution)/shard_map/all_gather | solution.py:131
  407.1 6.5 %copy.47 = bf16[2048,1024]{0,1:T(8,128)(2,1)} copy(bf16[2048,1024]{1,0:T(8,128)(2,1)} %all-gather.8.cloned.1.call-done) | data formatting | bytes 8388608 | tf_op jit(solution)/shard_map/all_gather | solution.py:131
  413.6 6.9 %fusion.11 = bf16[32,8,128]{2,0,1:T(8,128)(2,1)S(1)} fusion(bf16[2048,8,128]{0,2,1:T(8,128)(2,1)} %bitcast.66, f32[8,32,2048]{2,1,0:T(8,128)} %copy-done.1, f32[8,32]{1,0:T(8,128)S(1)} %broadcast_maximum_fusion, f32[32,8]{0,1:T(8,128)S(1)} %bitcast.76), kind=kOutput, calls=%fused_computation.16 | convolution fusion | flops 805896192 | bytes 6359040 | tf_op jit(solution)/shard_map/htn,nhd->htd/dot_general | solution.py:139
  (40 shorter events, 3.5 us)
Async XLA Ops:
  7.2 231.7 %copy-start = (bf16[2048,768]{1,0:T(8,128)(2,1)S(1)}, bf16[2048,768]{1,0:T(8,128)(2,1)}, u32[]{:S(2)}) copy-start(bf16[2048,768]{1,0:T(8,128)(2,1)} %param.25) | copy-start | bytes 9437188
  7.2 101.2 %all-gather.4.cloned.1.call-start = ((), (), s32[]{:S(2)}) async-start(), calls=%async_computation.4 | async-start | bytes 5242880 | tf_op jit(solution)/shard_map/all_gather | solution.py:61
  60.6 115.1 %reduce-scatter.2.cloned.1.call-start = ((), (), s32[]{:S(2)}) async-start(), calls=%async_computation.5 | async-start | bytes 5242880 | tf_op jit(solution)/shard_map/reduce_scatter | solution.py:68
  125.7 202.0 %all-gather.6.cloned.1.call-start = ((), (), s32[]{:S(2)}) async-start(), calls=%async_computation.6 | async-start | bytes 4259840 | tf_op jit(solution)/shard_map/all_gather | solution.py:130
  217.2 4.0 copy-start.2
  218.5 4.7 %copy-start.5 = (f32[2048]{0:T(1024)S(1)}, f32[2048]{0:T(1024)}, u32[]{:S(2)}) copy-start(f32[2048]{0:T(1024)} %param.20) | copy-start | bytes 24580
  218.5 6.0 %copy-start.3 = (f32[1,32,64]{2,1,0:T(8,128)S(1)}, f32[1,32,64]{2,1,0:T(8,128)}, u32[]{:S(2)}) copy-start(f32[1,32,64]{2,1,0:T(8,128)} %param.22) | copy-start | bytes 24580
  218.5 6.1 %copy-start.4 = (f32[1,2,2048]{2,1,0:T(2,128)S(1)}, f32[1,2,2048]{2,1,0:T(2,128)}, u32[]{:S(2)}) copy-start(f32[1,2,2048]{2,1,0:T(2,128)} %param.24) | copy-start | bytes 49156
  224.5 2.9 collective-permute-start
  248.2 158.9 %all-gather.8.cloned.1.call-start = ((), (), s32[]{:S(2)}) async-start(), calls=%async_computation.7 | async-start | bytes 4259840 | tf_op jit(solution)/shard_map/all_gather | solution.py:131
  337.1 1.4 copy-start.1
Sparse Core Ops, SparseCore 0:
  60.7 47.6 all-gather.3
  125.8 49.8 reduce-scatter.1
  248.3 79.2 all-gather.5
  330.9 76.2 all-gather.7
where the time goes:
time: 429 us; the launch traced here: 428 us
  waiting for transfers between devices  247 us (58%)
  blocking collectives  98.6 us (23%)
  matrix products  34.4 us (8%)
  local copies, waits for them, and re-layouts  27.6 us (6%)
  between operations  13.9 us (3%)
  other arithmetic  5.55 us (1%)
    all_gather x1, waiting for transfers between devices, per_device(): lax.all_gather(key_cols, 'ep', axis=0, tiled=True)  78.2 us
    all_gather x1, waiting for transfers between devices, per_device(): lax.all_gather(value_cols, 'ep', axis=0, tiled=True)  68.2 us
    reduce_scatter x1, waiting for transfers between devices, per_device(): lax.psum_scatter(jnp.dot(active, down_mat, preferred_element_type=jnp.flo...  50 us
    all_gather x1, waiting for transfers between devices, per_device(): lax.all_gather(arrived.reshape(-1, model_width), 'pair', axis=0, tiled=True)  47.7 us
    all_to_all x1, blocking collectives, per_device(): lax.all_to_all(doubled, 'ep', split_axis=0, concat_axis=0, tiled=True)  41.4 us
    all_to_all x1, blocking collectives, per_device(): lax.all_to_all(halves.reshape(2 * experts, capacity, model_width), 'ep',...  39.2 us
    dot_general x1, matrix products, per_device(): jnp.dot(active, down_mat, preferred_element_type=jnp.float32)  10.7 us
    all_gather x1, blocking collectives, per_device(): all_modulated = lax.all_gather(modulated, 'pair', axis=0, tiled=True)  9.92 us
  transfers between devices with their start and end apart: 5, of which 5 were waited for; matrix products, arithmetic and copies ran while one was open for 2% of the time, Pallas kernels for 0%

commit v1 on v0

v1 whole, which is shorter than its diff:
```python
import math

import jax
import jax.numpy as jnp
from jax import lax
from jax.experimental import pallas as pl
from jax.experimental.pallas import tpu as pltpu
from jax.sharding import Mesh
from jax.sharding import PartitionSpec as P

HDIM = 128
EPSILON = 1e-06
GUIDANCE = 3.0
STEP_SIZE = 0.25
CAP = 4
EP = ("x", "z", "core")
F32 = jnp.float32
BF16 = jnp.bfloat16
VMEM_LIMIT = 60 * 1024 * 1024


def vmem():
    return pl.BlockSpec(memory_space=pltpu.VMEM)


def slot_pick(ids_t, rows, frames):
    row = lax.broadcasted_iota(jnp.int32, (rows, frames), 0)
    expert = row >> 3
    slot = (row & (CAP - 1)).astype(F32)
    first = ids_t[0:1, :] == expert
    second = ids_t[1:2, :] == expert
    member = jnp.where(first | second, 1.0, 0.0)
    earlier = lax.broadcasted_iota(jnp.int32, (frames, frames), 0) < lax.broadcasted_iota(
        jnp.int32, (frames, frames), 1
    )
    rank = jnp.dot(
        member.astype(BF16), jnp.where(earlier, 1.0, 0.0).astype(BF16), preferred_element_type=F32
    )
    taken = (member > 0.0) & (rank == slot)
    return taken, first


def front_kernel(hidden_ref, gain_ref, ids_ref, out_ref):
    hidden = hidden_ref[...]
    frames, width = hidden.shape
    half = width // 2
    rows = out_ref.shape[0]
    mean = jnp.mean(hidden * hidden, -1, keepdims=True)
    normed = (hidden * lax.rsqrt(mean + EPSILON) * gain_ref[...]).astype(BF16)
    taken, _ = slot_pick(ids_ref[...], rows, frames)
    pick = jnp.where(taken, 1.0, 0.0).astype(BF16)
    low = jnp.dot(pick, normed[:, :half], preferred_element_type=F32)
    high = jnp.dot(pick, normed[:, half:], preferred_element_type=F32)
    row = lax.broadcasted_iota(jnp.int32, (rows, 1), 0)
    out_ref[...] = jnp.where((row & CAP) == 0, low, high).astype(BF16)


def expert_kernel(rows_ref, gate_ref, up_ref, down_ref, out_ref):
    rows = rows_ref[...]
    gated = jnp.dot(rows, gate_ref[...], preferred_element_type=F32)
    upward = jnp.dot(rows, up_ref[...], preferred_element_type=F32)
    active = (gated * jax.nn.sigmoid(gated) * upward).astype(BF16)
    out_ref[...] = jnp.dot(active, down_ref[...], preferred_element_type=F32).astype(BF16)


def experts(all_rows, gate_mat, up_mat, down_mat, block):
    total, width = all_rows.shape
    quarter = gate_mat.shape[1]
    return pl.pallas_call(
        expert_kernel,
        grid=(total // block,),
        in_specs=[
            pl.BlockSpec((block, width), lambda i: (i, 0)),
            pl.BlockSpec((width, quarter), lambda i: (0, 0)),
            pl.BlockSpec((width, quarter), lambda i: (0, 0)),
            pl.BlockSpec((quarter, width), lambda i: (0, 0)),
        ],
        out_specs=pl.BlockSpec((block, width), lambda i: (i, 0)),
        out_shape=jax.ShapeDtypeStruct((total, width), BF16),
        compiler_params=pltpu.CompilerParams(vmem_limit_bytes=VMEM_LIMIT),
        name="experts",
    )(all_rows, gate_mat, up_mat, down_mat)


def combine_kernel(back_ref, ids_ref, gates_ref, hidden_ref, gain_ref, w_out_ref, out_ref):
    hidden = hidden_ref[...]
    frames, width = hidden.shape
    half = width // 2
    rows = back_ref.shape[0]
    taken, first = slot_pick(ids_ref[...], rows, frames)
    weight = jnp.where(first, gates_ref[0:1, :], gates_ref[1:2, :])
    weight = jnp.where(taken, weight, 0.0)
    row = lax.broadcasted_iota(jnp.int32, (rows, frames), 0)
    back = back_ref[...]

    def gather(mat):
        top = mat.astype(BF16)
        rest = mat - top.astype(F32)
        mid = rest.astype(BF16)
        last = (rest - mid.astype(F32)).astype(BF16)
        dims = (((0,), (0,)), ((), ()))
        total = lax.dot_general(last, back, dims, preferred_element_type=F32)
        total = total + lax.dot_general(mid, back, dims, preferred_element_type=F32)
        return total + lax.dot_general(top, back, dims, preferred_element_type=F32)

    low = gather(jnp.where((row & CAP) == 0, weight, 0.0))
    high = gather(jnp.where((row & CAP) == 0, 0.0, weight))
    resid = hidden + jnp.concatenate([low, high], 1)
    mean = jnp.mean(resid * resid, -1, keepdims=True)
    scaled = (resid * lax.rsqrt(mean + EPSILON) * gain_ref[...]).astype(BF16)
    out_ref[...] = jnp.dot(scaled, w_out_ref[...], preferred_element_type=F32)


def attend_kernel(
    where_ref, adv_ref, w_in_ref, mod_ref, w_head_ref, out_ref, key_ref, value_ref, query_ref
):
    frames = adv_ref.shape[0]
    tok = 32
    block = 256
    w_in = w_in_ref[...]
    shift = mod_ref[0:1, :]
    scale = mod_ref[1:2, :]

    def modulate(adv):
        embedded = jnp.dot(adv, w_in, preferred_element_type=F32)
        mean = jnp.mean(embedded * embedded, -1, keepdims=True)
        return (embedded * lax.rsqrt(mean + EPSILON) * scale + shift).astype(BF16)

    pos = where_ref[0]
    for part in range(8):
        start = pl.multiple_of((part // 2) * 512 + pos * 64 + (part % 2) * tok, tok)
        query_ref[part * tok : (part + 1) * tok, :] = adv_ref[pl.ds(start, tok), :]
    query = jnp.dot(
        modulate(query_ref[...]), w_head_ref[where_ref[1]], preferred_element_type=F32
    ).astype(BF16)
    w_key = w_head_ref[where_ref[2]]
    w_value = w_head_ref[where_ref[3]]
    for i in range(frames // block):
        rows = modulate(adv_ref[i * block : (i + 1) * block, :])
        key_ref[i * block : (i + 1) * block, :] = jnp.dot(
            rows, w_key, preferred_element_type=F32
        ).astype(BF16)
        value_ref[i * block : (i + 1) * block, :] = jnp.dot(
            rows, w_value, preferred_element_type=F32
        ).astype(BF16)
    scores = lax.dot_general(
        query, key_ref[...], (((1,), (1,)), ((), ())), preferred_element_type=F32
    ) * (1.0 / math.sqrt(HDIM))
    weights = jnp.exp(scores - jnp.max(scores, 1, keepdims=True))
    total = jnp.sum(weights, 1, keepdims=True)
    mixed = jnp.dot(weights.astype(BF16), value_ref[...], preferred_element_type=F32)
    out_ref[...] = (mixed / total).astype(BF16)


def per_device(
    hidden,
    moe_gain,
    expert_ids,
    gate_weights,
    w_gate,
    w_up,
    w_down,
    final_gain,
    w_out,
    latent,
    w_in,
    modulation,
    w_qkv,
):
    tok_rows, width = hidden.shape[1:]
    n_chip = lax.axis_size("x") * lax.axis_size("z")
    n_pair = lax.axis_size("pair")
    own_hidden = hidden[0]
    ids_t = expert_ids[0].T
    gates_t = gate_weights[0].T
    gain_row = moe_gain.reshape(1, width)
    pair = lax.axis_index("pair")
    swap = [(i, i ^ 1) for i in range(n_pair)]

    head = lax.axis_index("x") * 2 + lax.axis_index("core")
    per_pair = w_qkv.shape[1] // HDIM
    n_head = n_pair * per_pair // 3
    ahead = (per_pair * pair - head + n_head - 1) // n_head
    local = jnp.clip(head + n_head * ahead - per_pair * pair, 0, per_pair - 1)
    w_mine = lax.dynamic_slice(w_qkv, (0, local * HDIM), (width, HDIM))
    w_head = lax.all_gather(w_mine, "pair", axis=0, tiled=False)
    where = jnp.stack(
        [
            lax.axis_index("z"),
            head // per_pair,
            (head + n_head) // per_pair,
            (head + 2 * n_head) // per_pair,
        ]
    ).astype(jnp.int32)

    rows = 2 * CAP * n_chip
    buffers = pl.pallas_call(
        front_kernel,
        in_specs=[vmem(), vmem(), vmem()],
        out_specs=vmem(),
        out_shape=jax.ShapeDtypeStruct((rows, width // 2), BF16),
        name="front",
    )(own_hidden, gain_row, ids_t)
    arrived = lax.all_to_all(buffers, ("x", "z"), split_axis=0, concat_axis=0, tiled=True)
    slots = n_chip * CAP
    out_row = lax.broadcasted_iota(jnp.int32, (slots, rows), 0)
    in_row = lax.broadcasted_iota(jnp.int32, (slots, rows), 1)
    low_at = (out_row // CAP) * 2 * CAP + out_row % CAP
    low_pick = (in_row == low_at).astype(BF16)
    high_pick = (in_row == low_at + CAP).astype(BF16)
    own_rows = jnp.concatenate(
        [
            jnp.dot(low_pick, arrived, preferred_element_type=F32).astype(BF16),
            jnp.dot(high_pick, arrived, preferred_element_type=F32).astype(BF16),
        ],
        1,
    )
    all_rows = lax.all_gather(own_rows, ("pair", "core"), axis=0, tiled=True)
    partial = experts(all_rows, w_gate[0], w_up[0], w_down[0], 256)
    summed = lax.psum_scatter(partial, ("pair", "core"), scatter_dimension=0, tiled=True)
    split = jnp.dot(low_pick.T, summed[:, : width // 2], preferred_element_type=F32) + jnp.dot(
        high_pick.T, summed[:, width // 2 :], preferred_element_type=F32
    )
    back = lax.all_to_all(
        split.astype(BF16), ("x", "z"), split_axis=0, concat_axis=0, tiled=True
    )
    velocity = pl.pallas_call(
        combine_kernel,
        in_specs=[vmem()] * 6,
        out_specs=vmem(),
        out_shape=jax.ShapeDtypeStruct((tok_rows, w_out.shape[1]), F32),
        name="combine",
    )(back, ids_t, gates_t, own_hidden, final_gain.reshape(1, width), w_out)

    own_latent = latent[0]
    partner_latent = lax.ppermute(own_latent, "pair", swap)
    partner_vel = lax.ppermute(velocity, "pair", swap)
    is_cond = pair % 2 == 0
    cond_vel = jnp.where(is_cond, velocity, partner_vel)
    uncond_vel = jnp.where(is_cond, partner_vel, velocity)
    guided = uncond_vel + GUIDANCE * (cond_vel - uncond_vel)
    whole_latent = jnp.where(
        is_cond,
        jnp.concatenate([own_latent, partner_latent], 1),
        jnp.concatenate([partner_latent, own_latent], 1),
    )
    advanced = whole_latent + STEP_SIZE * guided
    half_width = own_latent.shape[1]
    own_next = jnp.where(is_cond, advanced[:, :half_width], advanced[:, half_width:])

    copies = jnp.broadcast_to(
        advanced.astype(BF16)[None], (lax.axis_size(EP),) + advanced.shape
    ).reshape(-1, advanced.shape[1])
    all_adv = lax.all_to_all(copies, EP, split_axis=0, concat_axis=0, tiled=True)
    frames = all_adv.shape[0]
    queries = n_head * tok_rows
    mixed = pl.pallas_call(
        attend_kernel,
        in_specs=[pl.BlockSpec(memory_space=pltpu.SMEM)] + [vmem()] * 4,
        out_specs=vmem(),
        out_shape=jax.ShapeDtypeStruct((queries, HDIM), BF16),
        scratch_shapes=[
            pltpu.VMEM((frames, HDIM), BF16),
            pltpu.VMEM((frames, HDIM), BF16),
            pltpu.VMEM((queries, advanced.shape[1]), BF16),
        ],
        compiler_params=pltpu.CompilerParams(vmem_limit_bytes=VMEM_LIMIT),
        name="attend",
    )(where, all_adv, w_in, modulation[0], w_head)
    heads = lax.all_to_all(mixed, ("x", "core"), split_axis=0, concat_axis=0, tiled=True)
    attended = heads.reshape(n_head, tok_rows, HDIM).transpose(1, 0, 2).reshape(tok_rows, -1)
    return (own_next[None], attended[None])


def solution(mesh):
    chips = Mesh(mesh.devices.reshape(4, 4, 8, 2), ("pair", "x", "z", "core"))
    return jax.shard_map(
        per_device,
        mesh=chips,
        in_specs=(
            P("pair", EP, None),
            P(),
            P("pair", EP, None),
            P("pair", EP, None),
            P(EP, None, "pair"),
            P(EP, None, "pair"),
            P(EP, "pair", None),
            P(),
            P(),
            P("pair", EP, None),
            P(),
            P("pair", None, None),
            P(None, "pair"),
        ),
        out_specs=(P("pair", EP, None), P("pair", EP, None)),
        check_vma=False,
    )
```

time: 429 us -> 234 us (0.55)
  waiting for transfers between devices: 247 us -> 125 us
  blocking collectives: 98.6 us -> 22 us
  Pallas kernels: 0 us -> 29.8 us
  starting transfers between devices: 0.44 us -> 30.1 us
  matrix products: 34.4 us -> 5.57 us
  local copies, waits for them, and re-layouts: 27.6 us -> 2.4 us
    all_gather x3 -> x2, waiting for transfers between devices: 194 us -> 35 us  [the longest x1 35 us: per_device(): all_rows = lax.all_gather(own_rows, ('pair', 'core'), axis=0, tiled=True)]
    all_to_all x3 -> x1, blocking collectives: 88.6 us -> 22 us  [per_device(): lax.all_to_all(split.astype(BF16), ('x', 'z'), split_axis=0, concat_axis=...]
    all_to_all x0 -> x3, waiting for transfers between devices: none -> 35.1 us  [the longest x1 16.5 us: per_device(): lax.all_to_all(copies, EP, split_axis=0, concat_axis=0, tiled=True)]
    pallas_call x0 -> x4, Pallas kernels: none -> 29.8 us  [the longest x1 12.5 us: per_device(): pl.pallas_call(attend_kernel, in_specs=[pl.BlockSpec(memory_space=pltpu.S...]
    dot_general x9 -> x4, matrix products: 34.4 us -> 5.57 us  [the longest x1 1.42 us: per_device(): jnp.dot(high_pick.T, summed[:, width // 2:], preferred_element_type=F32)]
    all_to_all x0 -> x3, starting transfers between devices: none -> 24.1 us  [the longest x1 12 us: per_device(): lax.all_to_all(buffers, ('x', 'z'), split_axis=0, concat_axis=0, tiled=True)]
    all_gather x2 -> x0, local copies, waits for them, and re-layouts: 13 us -> none  [the longest x1 6.52 us: per_device(): lax.all_gather(value_cols, 'ep', axis=0, tiled=True)]
    all_gather x1 -> x0, blocking collectives: 9.92 us -> none  [per_device(): all_modulated = lax.all_gather(modulated, 'pair', axis=0, tiled=True)]
  transfers between devices with their start and end apart: 5 -> 8, of which waited for: 5 -> 6; matrix products, arithmetic and copies ran while one was open for 2% -> 3% of each run, Pallas kernels for 0% -> 1%
where the time goes in v1:
time: 234 us; the launch traced here: 233 us
  waiting for transfers between devices  125 us (53%)
  starting transfers between devices  30.1 us (13%)
  Pallas kernels  29.8 us (13%)
  blocking collectives  22 us (9%)
  between operations  15.7 us (7%)
  matrix products  5.57 us (2%)
  other arithmetic  2.98 us (1%)
  local copies, waits for them, and re-layouts  2.4 us (1%)
    reduce_scatter x1, waiting for transfers between devices, per_device(): lax.psum_scatter(partial, ('pair', 'core'), scatter_dimension=0, tiled=True)  51.7 us
    all_gather x1, waiting for transfers between devices, per_device(): all_rows = lax.all_gather(own_rows, ('pair', 'core'), axis=0, tiled=True)  35 us
    all_to_all x1, blocking collectives, per_device(): lax.all_to_all(split.astype(BF16), ('x', 'z'), split_axis=0, concat_axis=...  22 us
    all_to_all x1, waiting for transfers between devices, per_device(): lax.all_to_all(copies, EP, split_axis=0, concat_axis=0, tiled=True)  16.5 us
    all_to_all x1, waiting for transfers between devices, per_device(): lax.all_to_all(buffers, ('x', 'z'), split_axis=0, concat_axis=0, tiled=True)  14.4 us
    pallas_call x1, Pallas kernels, per_device(): pl.pallas_call(attend_kernel, in_specs=[pl.BlockSpec(memory_space=pltpu.S...  12.5 us
    all_to_all x1, starting transfers between devices, per_device(): lax.all_to_all(buffers, ('x', 'z'), split_axis=0, concat_axis=0, tiled=True)  12 us
    pallas_call x1, Pallas kernels, experts(): pl.pallas_call(expert_kernel, grid=(total // block,), in_specs=[pl.BlockS...  11.8 us
  transfers between devices with their start and end apart: 8, of which 6 were waited for; matrix products, arithmetic and copies ran while one was open for 3% of the time, Pallas kernels for 1%

profile of v1, /device:TPU:1, one launch (start us, length us, event | category | flops | bytes accessed | tf_op | source)
XLA Modules:
  0.0 233.3 jit_solution(12200741448956949331)
XLA Ops:
  8.0 2.5 %front.1 = bf16[256,1024]{1,0:T(8,128)(2,1)} custom-call(f32[32,2048]{1,0:T(8,128)} %bitcast.39, f32[1,2048]{1,0:T(1,128)} %bitcast.46, s32[2,32]{1,0:T(2,128)} %bitcast.48), custom_call_target="tpu_custom_call" | custom-call | tf_op jit(solution)/shard_map/front/pallas_call | solution.py:197
  10.5 12.0 %all-to-all-start = ((bf16[32,8,1024]{2,1,0:T(8,128)(2,1)}), bf16[32,8,1024]{2,1,0:T(8,128)(2,1)}, u32[]{:S(2)}, u32[]{:S(2)}) async-start(bf16[32,8,1024]{2,1,0:T(8,128)(2,1)} %bitcast.37), calls=%async_computation | async-start | bytes 1048576 | tf_op jit(solution)/shard_map/all_to_all | solution.py:204
  22.5 0.0 all-gather.4.cloned.1.call-start
  22.5 14.4 %all-to-all-done = bf16[32,8,1024]{2,1,0:T(8,128)(2,1)} async-done(((bf16[32,8,1024]{2,1,0:T(8,128)(2,1)}), bf16[32,8,1024]{2,1,0:T(8,128)(2,1)}, u32[]{:S(2)}, u32[]{:S(2)}) %all-to-all-start) | async-done | bytes 524320 | tf_op jit(solution)/shard_map/all_to_all | solution.py:204
  37.0 1.4 convolution_convert_fusion
  38.3 1.4 convolution_convert_fusion.1
  39.7 0.8 pad_maximum_fusion
  40.5 0.0 all-gather.4.cloned.1.call-update
  40.6 0.0 reduce-scatter.2.cloned.1.call-start
  40.6 35.0 %all-gather.4.cloned.1.call-done.rows_ref = bf16[1024,2048]{1,0:T(8,128)(2,1)} async-done(((bf16[128,2048]{1,0:T(8,128)(2,1)}), bf16[1024,2048]{1,0:T(8,128)(2,1)}) %all-gather.4.cloned.1.call-update) | async-done | bytes 4194320 | tf_op jit(solution)/shard_map/all_gather | solution.py:218
  75.6 11.8 %experts.1 = bf16[1024,2048]{1,0:T(8,128)(2,1)} custom-call(bf16[1024,2048]{1,0:T(8,128)(2,1)} %all-gather.4.cloned.1.call-done.rows_ref, bf16[2048,512]{1,0:T(8,128)(2,1)} %bitcast.33, bf16[2048,512]{1,0:T(8,128)(2,1)} %bitcast.34, bf16[512,2048]{1,0:T(8,128)(2,1)} %bitcast.35), custom_call_target="tpu_custom_call" | custom-call | tf_op jit(solution)/shard_map/experts/pallas_call | solution.py:69
  87.4 0.0 all-gather.6.cloned.1.call-start
  87.5 0.8 constant_dynamic-slice_fusion
  88.3 0.0 all-gather.6.cloned.1.call-update
  88.4 51.7 %reduce-scatter.2.cloned.1.call-done = bf16[128,2048]{1,0:T(8,128)(2,1)} async-done(((bf16[1024,2048]{1,0:T(8,128)(2,1)}), bf16[128,2048]{1,0:T(8,128)(2,1)}) %reduce-scatter.2.cloned.1.call-update) | async-done | bytes 524304 | tf_op jit(solution)/shard_map/reduce_scatter | solution.py:220
  140.1 1.4 fusion.5
  141.5 1.4 fusion.1
  142.9 22.0 %all_to_all.40 = bf16[32,8,1024]{2,1,0:T(8,128)(2,1)} all-to-all(bf16[32,8,1024]{2,1,0:T(8,128)(2,1)S(1)} %fusion.1), channel_id=1, replica_groups=mesh['pair'=4,'x'=4,'z'=8,'core'=2] {'x','z'}, dimensions={0} | all-to-all | bytes 1048576 | tf_op jit(solution)/shard_map/all_to_all | solution.py:224
  164.9 3.1 %combine.1 = f32[32,128]{1,0:T(8,128)} custom-call(bf16[256,1024]{1,0:T(8,128)(2,1)} %bitcast.38, s32[2,32]{1,0:T(2,128)} %bitcast.49, f32[2,32]{1,0:T(2,128)} %bitcast.50, f32[32,2048]{1,0:T(8,128)} %bitcast.40, f32[1,2048]{1,0:T(1,128)} %bitcast.47, bf16[2048,128]{1,0:T(8,128)(2,1)} %w_out_ref.1), custom_call_target="tpu_custom_call" | custom-call | tf_op jit(solution)/shard_map/combine/pallas_call | solution.py:227
  168.0 5.9 %collective-permute-start.1 = (f32[32,128]{1,0:T(8,128)}, f32[32,128]{1,0:T(8,128)S(1)}, u32[]{:S(2)}, u32[]{:S(2)}) collective-permute-start(f32[32,128]{1,0:T(8,128)} %combine.1), channel_id=1, source_target_pairs={{0,64},{64,0},{128,192},{192,128},{1,65},{65,1},{129,193},{193,129... | collective-permute-start | bytes 49160 | tf_op jit(solution)/shard_map/ppermute | solution.py:237
  173.8 0.1 collective-permute-start
  173.9 2.9 %collective-permute-done = f32[32,64]{1,0:T(8,128)S(1)} collective-permute-done((f32[32,64]{1,0:T(8,128)S(1)}, f32[32,64]{1,0:T(8,128)S(1)}, u32[]{:S(2)}, u32[]{:S(2)}) %collective-permute-start) | collective-permute-done | bytes 8224 | tf_op jit(solution)/shard_map/ppermute | solution.py:236
  176.8 0.8 fusion.12
  177.6 0.9 broadcast_in_dim.10
  178.5 7.5 %all-to-all-start.2 = ((bf16[64,32,128]{2,1,0:T(8,128)(2,1)}), bf16[64,32,128]{2,1,0:T(8,128)(2,1)}, u32[]{:S(2)}, u32[]{:S(2)}) async-start(bf16[64,32,128]{2,1,0:T(8,128)(2,1)} %broadcast_in_dim.10), calls=%async_computation.3 | async-start | bytes 1048576 | tf_op jit(solution)/shard_map/all_to_all | solution.py:254
  186.1 0.7 pad_add_fusion.where_ref
  186.8 16.5 %all-to-all-done.2 = bf16[64,32,128]{2,1,0:T(8,128)(2,1)} async-done(((bf16[64,32,128]{2,1,0:T(8,128)(2,1)}), bf16[64,32,128]{2,1,0:T(8,128)(2,1)}, u32[]{:S(2)}, u32[]{:S(2)}) %all-to-all-start.2) | async-done | bytes 524320 | tf_op jit(solution)/shard_map/all_to_all | solution.py:254
  203.2 12.5 %attend.1 = bf16[256,128]{1,0:T(8,128)(2,1)} custom-call(s32[4]{0:T(128)} %pad_add_fusion.where_ref, bf16[2048,128]{1,0:T(8,128)(2,1)} %bitcast.20.adv_ref, bf16[128,2048]{1,0:T(8,128)(2,1)} %w_in_ref.1, f32[2,2048]{1,0:T(2,128)} %bitcast.43, bf16[4,2048,128]{2,1,0:T(8,128)(2,1)} %bitcast.36), custom_call_target="tpu_custom_call" | custom-call | tf_op jit(solution)/shard_map/attend/pallas_call | solution.py:257
  215.8 4.5 %all-to-all-start.3 = ((bf16[8,32,128]{2,1,0:T(8,128)(2,1)}), bf16[8,32,128]{2,1,0:T(8,128)(2,1)S(1)}, u32[]{:S(2)}, u32[]{:S(2)}) async-start(bf16[8,32,128]{2,1,0:T(8,128)(2,1)} %bitcast.41), calls=%async_computation.4 | async-start | bytes 131072 | tf_op jit(solution)/shard_map/all_to_all | solution.py:270
  220.3 0.7 fusion.8
  221.0 4.2 %all-to-all-done.3 = bf16[8,32,128]{2,1,0:T(8,128)(2,1)S(1)} async-done(((bf16[8,32,128]{2,1,0:T(8,128)(2,1)}), bf16[8,32,128]{2,1,0:T(8,128)(2,1)S(1)}, u32[]{:S(2)}, u32[]{:S(2)}) %all-to-all-start.3) | async-done | bytes 65568 | tf_op jit(solution)/shard_map/all_to_all | solution.py:270
  225.2 0.7 broadcast_in_dim_reshape.3
  (11 shorter events, 0.1 us)
Async XLA Ops:
  8.0 79.5 %copy-start = (bf16[2048,768]{1,0:T(8,128)(2,1)S(1)}, bf16[2048,768]{1,0:T(8,128)(2,1)}, u32[]{:S(2)}) copy-start(bf16[2048,768]{1,0:T(8,128)(2,1)} %param.25) | copy-start | bytes 9437188
  10.5 26.5 %all-to-all-start = ((bf16[32,8,1024]{2,1,0:T(8,128)(2,1)}), bf16[32,8,1024]{2,1,0:T(8,128)(2,1)}, u32[]{:S(2)}, u32[]{:S(2)}) async-start(bf16[32,8,1024]{2,1,0:T(8,128)(2,1)} %bitcast.37), calls=%async_computation | async-start | bytes 1048576 | tf_op jit(solution)/shard_map/all_to_all | solution.py:204
  22.5 53.2 %all-gather.4.cloned.1.call-start = ((), (), s32[]{:S(2)}) async-start(), calls=%async_computation.5 | async-start | bytes 4718592 | tf_op jit(solution)/shard_map/all_gather | solution.py:218
  40.6 99.5 %reduce-scatter.2.cloned.1.call-start = ((), (), s32[]{:S(2)}) async-start(), calls=%async_computation.6 | async-start | bytes 4718592 | tf_op jit(solution)/shard_map/reduce_scatter | solution.py:220
  87.4 99.4 %all-gather.6.cloned.1.call-start = ((), (), s32[]{:S(2)}) async-start(), calls=%async_computation.7 | async-start | bytes 2621440 | tf_op jit(solution)/shard_map/all_gather | solution.py:186
  88.3 85.5 %copy-start.1 = (f32[1,32,64]{2,1,0:T(8,128)S(1)}, f32[1,32,64]{2,1,0:T(8,128)}, u32[]{:S(2)}) copy-start(f32[1,32,64]{2,1,0:T(8,128)} %param.22) | copy-start | bytes 24580
  168.0 8.9 %collective-permute-start.1 = (f32[32,128]{1,0:T(8,128)}, f32[32,128]{1,0:T(8,128)S(1)}, u32[]{:S(2)}, u32[]{:S(2)}) collective-permute-start(f32[32,128]{1,0:T(8,128)} %combine.1), channel_id=1, source_target_pairs={{0,64},{64,0},{128,192},{192,128},{1,65},{65,1},{129,193},{193,129... | collective-permute-start | bytes 49160 | tf_op jit(solution)/shard_map/ppermute | solution.py:237
  173.8 3.0 %collective-permute-start = (f32[32,64]{1,0:T(8,128)S(1)}, f32[32,64]{1,0:T(8,128)S(1)}, u32[]{:S(2)}, u32[]{:S(2)}) collective-permute-start(f32[32,64]{1,0:T(8,128)S(1)} %bitcast.44), channel_id=1, source_target_pairs={{0,64},{64,0},{128,192},{192,128},{1,65},{65,1},{129,193},{193,129... | collective-permute-start | bytes 24584 | tf_op jit(solution)/shard_map/ppermute | solution.py:236
  178.5 24.7 %all-to-all-start.2 = ((bf16[64,32,128]{2,1,0:T(8,128)(2,1)}), bf16[64,32,128]{2,1,0:T(8,128)(2,1)}, u32[]{:S(2)}, u32[]{:S(2)}) async-start(bf16[64,32,128]{2,1,0:T(8,128)(2,1)} %broadcast_in_dim.10), calls=%async_computation.3 | async-start | bytes 1048576 | tf_op jit(solution)/shard_map/all_to_all | solution.py:254
  215.8 9.4 %all-to-all-start.3 = ((bf16[8,32,128]{2,1,0:T(8,128)(2,1)}), bf16[8,32,128]{2,1,0:T(8,128)(2,1)S(1)}, u32[]{:S(2)}, u32[]{:S(2)}) async-start(bf16[8,32,128]{2,1,0:T(8,128)(2,1)} %bitcast.41), calls=%async_computation.4 | async-start | bytes 131072 | tf_op jit(solution)/shard_map/all_to_all | solution.py:270
Sparse Core Ops, SparseCore 0:
  40.7 34.9 all-gather.3
  87.5 52.4 reduce-scatter.1
Sparse Core Ops, SparseCore 1:
  89.7 38.7 all-gather.5
